TPU v7x, 32 devices: a whole 2x2x4 slice. The times are simulated.
32 devices in a mesh: dp: 4 (over z), ctx: 8 (over y, x, core).
Axes of the slice: x: 2, y: 2, z: 4, core: 2. Of those that a mesh axis runs over, the one named last changes fastest.
Arguments:
- queries: bfloat16 [4, 1024, 1024], P('dp', 'ctx'), may hold values from -6 to 6
- keys: bfloat16 [4, 1024, 1024], P('dp', 'ctx'), may hold values from -6 to 6
- values: bfloat16 [4, 1024, 1024], P('dp', 'ctx'), may hold values from -6 to 6
- outputs: bfloat16 [4, 1024, 1024], P('dp', 'ctx'), may hold values from -1.25 to 1.25
- d_out: bfloat16 [4, 1024, 1024], P('dp', 'ctx'), may hold values from -6 to 6
- lse: float32 [4, 16, 1024], P('dp', None, 'ctx'), may hold values from 3 to 5
- glob_keys: bfloat16 [128, 1024], replicated, may hold values from -6 to 6
- glob_values: bfloat16 [128, 1024], replicated, may hold values from -6 to 6
- rand_owner: int32 [16, 3], P('ctx'), may hold values from 0 to 7, all different within a row; in each aligned block of 2 rows (0 to 1, 2 to 3, ...) at most 2 rows name the same one
- rand_local: int32 [16, 3], P('ctx'), may hold values from 0 to 1
Outputs:
- d_queries: bfloat16 [4, 1024, 1024], P('dp', 'ctx')
- d_keys: bfloat16 [4, 1024, 1024], P('dp', 'ctx')
- d_values: bfloat16 [4, 1024, 1024], P('dp', 'ctx')
- d_glob_keys: float32 [128, 1024], replicated
- d_glob_values: float32 [128, 1024], replicated
Inputs may be any that keep to these rules, and one draw needn't show every extreme that they name: `rand_owner`: the 3 random blocks of one query block lie on different ctx indices. Among the 2 query blocks of one device no ctx index is named more than 2 times.
All inputs are finite; a program needn't handle non-finite values.
Results may differ from a plain program's by a relative error of at most 0.0055.
Values may be sent and summed in bfloat16 or wider, within the bound.
A program may use at most 128 MiB of HBM per device.

v0:
```python
import jax
import jax.numpy as jnp
from jax import lax
from jax.sharding import PartitionSpec as P

HEADS = 16
HDIM = 64
BLK = 64
GLOB = 128


def extended(block, sides, width):
    for axis, dim in sides:
        count = lax.axis_size(axis)
        forward = [(i, i + 1) for i in range(count - 1)]
        forward.append((count - 1, 0))
        backward = [(target, source) for source, target in forward]
        low = lax.ppermute(
            lax.slice_in_dim(block, block.shape[dim] - width, None, axis=dim), axis, forward
        )
        high = lax.ppermute(lax.slice_in_dim(block, 0, width, axis=dim), axis, backward)
        block = jnp.concatenate([low, block, high], axis=dim)
    return block


def block_grads(query_blk, dout_blk, lse_blk, delta_blk, key_blk, value_blk):
    scaling = HDIM ** (-0.5)
    scores = (
        jnp.einsum("nqhe,nkhe->nhqk", query_blk, key_blk, preferred_element_type=jnp.float32)
        * scaling
    )
    probability = jnp.exp(scores - lse_blk[..., None])
    prob_low = probability.astype(jnp.bfloat16)
    d_probability = jnp.einsum(
        "nqhe,nkhe->nhqk", dout_blk, value_blk, preferred_element_type=jnp.float32
    )
    d_scores = (probability * (d_probability - delta_blk[..., None])).astype(jnp.bfloat16)
    grad_q = (
        jnp.einsum("nhqk,nkhe->nqhe", d_scores, key_blk, preferred_element_type=jnp.float32)
        * scaling
    )
    grad_k = (
        jnp.einsum("nhqk,nqhe->nkhe", d_scores, query_blk, preferred_element_type=jnp.float32)
        * scaling
    )
    grad_v = jnp.einsum("nhqk,nqhe->nkhe", prob_low, dout_blk, preferred_element_type=jnp.float32)
    return (grad_q, grad_k, grad_v)


def spread_window(section):
    pad_rest = ((0, 0), (0, 0), (0, 0))
    lower = jnp.pad(section[:, :BLK], ((0, 2),) + pad_rest)
    middle = jnp.pad(section[:, BLK : 2 * BLK], ((1, 1),) + pad_rest)
    upper = jnp.pad(section[:, 2 * BLK :], ((2, 0),) + pad_rest)
    return lower + middle + upper


def shards(
    queries, keys, values, outputs, d_out, lse, glob_keys, glob_values, rand_owner, rand_local
):
    tokens_dev = queries.shape[1]
    feature_dim = queries.shape[2]
    blocks = tokens_dev // BLK
    cycle_size = lax.axis_size("ctx")
    per_block = rand_owner.shape[1]
    pairs = blocks * per_block
    query_blk = queries.reshape(blocks, BLK, HEADS, HDIM)
    dout_blk = d_out.reshape(blocks, BLK, HEADS, HDIM)
    product = d_out.astype(jnp.float32) * outputs.astype(jnp.float32)
    delta_blk = jnp.sum(product.reshape(blocks, BLK, HEADS, HDIM), axis=3).transpose(0, 2, 1)
    lse_blk = lse.reshape(HEADS, blocks, BLK).transpose(1, 0, 2)
    key_value = jnp.stack([keys[0], values[0]])
    padded = extended(key_value, (("ctx", 1),), BLK)

    def split_blocks(section):
        return section.reshape(2, blocks, BLK, HEADS, HDIM)

    window = jnp.concatenate(
        [
            split_blocks(padded[:, :tokens_dev]),
            split_blocks(padded[:, BLK : BLK + tokens_dev]),
            split_blocks(padded[:, 2 * BLK :]),
        ],
        axis=2,
    )
    dq_win, dk_win, dv_win = block_grads(
        query_blk, dout_blk, lse_blk, delta_blk, window[0], window[1]
    )
    grad_grid = jnp.stack([spread_window(dk_win), spread_window(dv_win)]).reshape(
        2, tokens_dev + 2 * BLK, feature_dim
    )
    edge_rims = jnp.concatenate([grad_grid[:, :BLK], grad_grid[:, tokens_dev + BLK :]], axis=1)
    returned = extended(edge_rims, (("ctx", 1),), BLK)
    kv_grad = grad_grid[:, BLK : tokens_dev + BLK]
    kv_grad = kv_grad.at[:, :BLK].add(returned[:, :BLK])
    kv_grad = kv_grad.at[:, tokens_dev - BLK :].add(returned[:, 3 * BLK :])
    mem_keys = jnp.broadcast_to(
        glob_keys.reshape(1, GLOB, HEADS, HDIM), (blocks, GLOB, HEADS, HDIM)
    )
    mem_values = jnp.broadcast_to(
        glob_values.reshape(1, GLOB, HEADS, HDIM), (blocks, GLOB, HEADS, HDIM)
    )
    dq_mem, dk_mem, dv_mem = block_grads(
        query_blk, dout_blk, lse_blk, delta_blk, mem_keys, mem_values
    )
    mem_terms = jnp.stack([jnp.sum(dk_mem, axis=0), jnp.sum(dv_mem, axis=0)]).reshape(
        2, GLOB, feature_dim
    )
    memory_total = lax.psum(mem_terms, ("dp", "ctx"))
    capacity = min(blocks, max(2, 2 * blocks * per_block // cycle_size))
    owner_flat = rand_owner.reshape(-1)
    local_flat = rand_local.reshape(-1)
    owner_hits = (owner_flat[:, None] == jnp.arange(cycle_size, dtype=jnp.int32)[None, :]).astype(
        jnp.int32
    )
    earlier = jnp.cumsum(owner_hits, axis=0) - owner_hits
    slot_rank = jnp.sum(earlier * owner_hits, axis=1)
    slot_index = owner_flat * capacity + slot_rank
    wanted = (
        jnp.zeros((cycle_size * capacity,), jnp.int32)
        .at[slot_index]
        .set(local_flat)
        .reshape(cycle_size, capacity)
    )
    kv_blocks = jnp.stack(
        [keys[0].reshape(blocks, BLK, feature_dim), values[0].reshape(blocks, BLK, feature_dim)],
        axis=1,
    )
    query_pairs = jnp.repeat(query_blk, per_block, axis=0)
    dout_pairs = jnp.repeat(dout_blk, per_block, axis=0)
    lse_pairs = jnp.repeat(lse_blk, per_block, axis=0)
    delta_pairs = jnp.repeat(delta_blk, per_block, axis=0)
    slots_all = cycle_size * capacity
    asked_ids = lax.all_to_all(wanted, "ctx", split_axis=0, concat_axis=0, tiled=True)
    picked = kv_blocks[asked_ids]
    fetched, asked_ids = (
        lax.all_to_all(picked, "ctx", split_axis=0, concat_axis=0, tiled=True),
        asked_ids,
    )
    chosen = fetched.reshape(slots_all, 2, BLK, HEADS, HDIM)[slot_index]
    dq_pair, dk_pair, dv_pair = block_grads(
        query_pairs, dout_pairs, lse_pairs, delta_pairs, chosen[:, 0], chosen[:, 1]
    )
    dq_rand = lax.optimization_barrier(dq_pair.astype(jnp.bfloat16)).astype(jnp.float32)
    pair_grads = (
        jnp.stack([dk_pair, dv_pair], axis=1)
        .reshape(pairs, 2, BLK, feature_dim)
        .astype(jnp.bfloat16)
    )
    grad_slots = (
        jnp.zeros((slots_all, 2, BLK, feature_dim), jnp.bfloat16).at[slot_index].set(pair_grads)
    )
    arrived = lax.all_to_all(
        grad_slots.reshape(cycle_size, capacity, 2, BLK, feature_dim),
        "ctx",
        split_axis=0,
        concat_axis=0,
        tiled=True,
    )
    received = arrived.reshape(slots_all, 2, BLK, feature_dim)
    kv_rand = (
        jnp.zeros((blocks, 2, BLK, feature_dim), jnp.float32)
        .at[asked_ids.reshape(-1)]
        .add(received.astype(jnp.float32))
    )
    dq_rand_sum = jnp.sum(dq_rand.reshape(blocks, per_block, BLK, HEADS, HDIM), axis=1)
    grad_queries = (
        (dq_win + dq_mem + dq_rand_sum).reshape(1, tokens_dev, feature_dim).astype(jnp.bfloat16)
    )
    grad_keys = (
        (kv_grad[0] + kv_rand[:, 0].reshape(tokens_dev, feature_dim))
        .reshape(1, tokens_dev, feature_dim)
        .astype(jnp.bfloat16)
    )
    grad_values = (
        (kv_grad[1] + kv_rand[:, 1].reshape(tokens_dev, feature_dim))
        .reshape(1, tokens_dev, feature_dim)
        .astype(jnp.bfloat16)
    )
    return (grad_queries, grad_keys, grad_values, memory_total[0], memory_total[1])


def solution(mesh):
    return jax.shard_map(
        shards,
        mesh=mesh,
        in_specs=(
            P("dp", "ctx", None),
            P("dp", "ctx", None),
            P("dp", "ctx", None),
            P("dp", "ctx", None),
            P("dp", "ctx", None),
            P("dp", None, "ctx"),
            P(),
            P(),
            P("ctx", None),
            P("ctx", None),
        ),
        out_specs=(P("dp", "ctx", None), P("dp", "ctx", None), P("dp", "ctx", None), P(), P()),
        check_vma=False,
    )
```

profile of v0, /device:TPU:0, one launch (start us, length us, event | category | flops | bytes accessed | tf_op | source)
XLA Modules:
  0.0 246.8 jit_solution(17565777443147992249)
XLA Ops:
  11.0 5.2 %all-to-all-start = ((s32[8,1,2]{2,1,0:T(1,128)}), s32[8,1,2]{2,1,0:T(1,128)S(1)}, u32[]{:S(2)}, u32[]{:S(2)}) async-start(s32[8,1,2]{2,1,0:T(1,128)} %bitcast.12), calls=%async_computation | async-start | bytes 8192 | tf_op jit(solution)/shard_map/all_to_all | solution.py:134
  17.3 3.5 %all-to-all-done = s32[8,1,2]{2,1,0:T(1,128)S(1)} async-done(((s32[8,1,2]{2,1,0:T(1,128)}), s32[8,1,2]{2,1,0:T(1,128)S(1)}, u32[]{:S(2)}, u32[]{:S(2)}) %all-to-all-start) | async-done | bytes 96 | tf_op jit(solution)/shard_map/all_to_all | solution.py:134
  21.0 2.8 %gather_fusion = bf16[16,2,64,1024]{3,2,1,0:T(8,128)(2,1)} fusion(bf16[2,2,64,1024]{3,2,0,1:T(8,128)(2,1)S(1)} %pad_maximum_fusion.5, s32[1024]{0:T(1024)S(1)} %pad_clamp_fusion.1), kind=kCustom, calls=%fused_computation | custom fusion | bytes 8388672 | tf_op jit(solution)/shard_map/gather | solution.py:135
  23.8 4.7 %all-to-all-start.1 = ((bf16[8,2,2,64,1024]{4,3,2,1,0:T(8,128)(2,1)}), bf16[8,2,2,64,1024]{4,3,2,1,0:T(8,128)(2,1)}, u32[]{:S(2)}, u32[]{:S(2)}) async-start(bf16[8,2,2,64,1024]{4,3,2,1,0:T(8,128)(2,1)} %bitcast.105), calls=%async_computation.1 | async-start | bytes 8388608 | tf_op jit(solution)/shard_map/all_to_all | solution.py:137
  29.9 2.3 collective-permute-start.1
  45.7 39.9 %collective-permute-done = bf16[2,64,1024]{2,1,0:T(8,128)(2,1)} collective-permute-done((bf16[2,64,1024]{2,1,0:T(8,128)(2,1)}, bf16[2,64,1024]{2,1,0:T(8,128)(2,1)}, u32[]{:S(2)}, u32[]{:S(2)}) %collective-permute-start) | collective-permute-done | bytes 262176 | tf_op jit(solution)/shard_map/ppermute | solution.py:18
  87.5 2.5 %reshape.256 = bf16[2,2,64,16,64]{4,3,2,1,0:T(8,128)(2,1)} reshape(bf16[2,128,1024]{2,1,0:T(8,128)(2,1)} %get-tuple-element.66) | data formatting | bytes 1048576 | tf_op jit(solution)/shard_map/reshape | solution.py:76
  90.0 2.7 %copy.130 = bf16[2,2,64,16,64]{2,4,3,1,0:T(8,128)(2,1)} copy(bf16[2,2,64,16,64]{4,3,2,1,0:T(8,128)(2,1)} %reshape.256) | data formatting | bytes 1048576 | tf_op jit(solution)/shard_map/reshape | solution.py:76
  94.3 2.7 %copy.128 = bf16[2,2,64,16,64]{2,4,3,1,0:T(8,128)(2,1)} copy(bf16[2,2,64,16,64]{4,3,2,1,0:T(8,128)(2,1)} %reshape.254) | data formatting | bytes 1048576 | tf_op jit(solution)/shard_map/reshape | solution.py:76
  97.0 2.5 %pad_maximum_fusion = bf16[2,2,192,16,64]{2,4,3,1,0:T(8,128)(2,1)S(1)} fusion(bf16[2,2,64,16,64]{2,4,3,1,0:T(8,128)(2,1)} %copy.130, bf16[2,2,64,16,64]{2,4,3,1,0:T(8,128)(2,1)S(1)} %copy.129, bf16[2,2,64,16,64]{2,4,3,1,0:T(8,128)(2,1)} %copy.128), kind=kLoop, calls=%fused_computation.12 | loop fusion | flops 4718592 | bytes 3145728 | tf_op jit(solution)/shard_map/concatenate | solution.py:78
  104.3 11.6 %reshape.262 = bf16[16,2,64,16,64]{4,3,2,1,0:T(8,128)(2,1)} reshape(bf16[8,2,2,64,1024]{4,3,2,1,0:T(8,128)(2,1)} %all-to-all-done.1) | data formatting | bytes 8388608 | tf_op jit(solution)/shard_map/reshape | solution.py:140
  115.9 4.5 %gather_fusion.1 = bf16[6,2,64,16,64]{4,3,2,1,0:T(8,128)(2,1)S(1)} fusion(bf16[16,2,64,16,64]{4,3,2,1,0:T(8,128)(2,1)} %reshape.262, s32[1024]{0:T(1024)S(1)} %pad_clamp_fusion), kind=kCustom, calls=%fused_computation.1 | custom fusion | bytes 3145752 | tf_op jit(solution)/shard_map/gather | solution.py:140
  125.7 2.2 copy.156
  127.9 3.4 %stack.39 = bf16[6,1,64,1024]{3,2,0,1:T(8,128)(2,1)} reshape(bf16[6,64,16,64]{3,2,1,0:T(8,128)(2,1)} %copy.156) | data formatting | bytes 1572864 | tf_op jit(solution)/shard_map/stack | solution.py:146
  131.4 3.1 %multiply_convert_fusion.2 = bf16[6,16,64,64]{3,2,1,0:T(8,128)(2,1)S(1)} fusion(f32[6,16,64,64]{3,2,1,0:T(8,128)S(1)} %fusion.10, bf16[6,64,16,64]{3,1,2,0:T(8,128)(2,1)} %bitcast.109, bf16[6,1,64,16,64]{4,3,2,1,0:T(8,128)(2,1)} %get-tuple-element.49, f32[6,16,64]{2,1,0:T(8,128)S(1)} %bitcast.127, f32[6,16,64]{2,1,0:T(8,128)S(1)} %bitcast.121), kind=kOutput, calls=%fused_computation.9 | convolution fusion | flops 52297728 | bytes 3981312 | tf_op jit(solution)/shard_map/nqhe,nkhe->nhqk/dot_general | solution.py:34
  138.1 2.5 %broadcast_in_dim.51 = bf16[16,2,64,1024]{3,2,1,0:T(8,128)(2,1)} broadcast(bf16[]{:T(256)} %constant.82.clone.1), dimensions={} | broadcast | bytes 4194306 | tf_op jit(solution)/shard_map/broadcast_in_dim | solution.py:151
  140.6 4.8 %scatter_fusion = bf16[16,2,64,1024]{3,2,1,0:T(8,128)(2,1)} fusion(bf16[16,2,64,1024]{3,2,1,0:T(8,128)(2,1)} %broadcast_in_dim.51, s32[6]{0:T(128)S(1)} %fusion.34, bf16[6,2,64,1024]{3,2,1,0:T(8,128)(2,1)S(1)} %copy.157), kind=kCustom, calls=%fused_computation.3 | custom fusion | bytes 4718616 | tf_op jit(solution)/shard_map/scatter | solution.py:151
  145.4 5.0 %all-to-all-start.2 = ((bf16[8,2,2,64,1024]{4,3,2,1,0:T(8,128)(2,1)}), bf16[8,2,2,64,1024]{4,3,2,1,0:T(8,128)(2,1)}, u32[]{:S(2)}, u32[]{:S(2)}) async-start(bf16[8,2,2,64,1024]{4,3,2,1,0:T(8,128)(2,1)} %bitcast.104), calls=%async_computation.2 | async-start | bytes 8388608 | tf_op jit(solution)/shard_map/all_to_all | solution.py:153
  153.3 2.9 %stack.35 = f32[1,256,1024]{2,1,0:T(8,128)} reshape(f32[4,64,16,64]{3,2,1,0:T(8,128)} %copy.152) | data formatting | bytes 2097152 | tf_op jit(solution)/shard_map/stack | solution.py:89
  164.8 2.5 %collective-permute-start.3 = (f32[2,64,1024]{2,1,0:T(8,128)}, f32[2,64,1024]{2,1,0:T(8,128)}, u32[]{:S(2)}, u32[]{:S(2)}) collective-permute-start(f32[2,64,1024]{2,1,0:T(8,128)} %get-tuple-element.51), channel_id=1, source_target_pairs={{1,0},{2,1},{3,2},{4,3},{5,4},{6,5},{7,6},{0,7},{9,8},{10,9},{11,1... | collective-permute-start | bytes 1572872 | tf_op jit(solution)/shard_map/ppermute | solution.py:21
  168.8 10.2 %all-reduce.8.cloned.1.call-done = f32[2,128,1024]{1,2,0:T(8,128)} async-done(((f32[2,128,1024]{1,2,0:T(8,128)}), f32[2,128,1024]{1,2,0:T(8,128)}) %all-reduce.8.cloned.1.call-update) | async-done | bytes 1048592 | tf_op jit(solution)/shard_map/psum | solution.py:109
  184.3 27.9 %collective-permute-done.2 = f32[2,64,1024]{2,1,0:T(8,128)} collective-permute-done((f32[2,64,1024]{2,1,0:T(8,128)}, f32[2,64,1024]{2,1,0:T(8,128)}, u32[]{:S(2)}, u32[]{:S(2)}) %collective-permute-start.2) | collective-permute-done | bytes 524320 | tf_op jit(solution)/shard_map/ppermute | solution.py:18
  220.4 6.5 %bitcast_convert_fusion = f32[16,2,64,1024]{3,2,1,0:T(8,128)} fusion(bf16[8,2,2,64,1024]{4,3,2,1,0:T(8,128)(2,1)} %all-to-all-done.2), kind=kLoop, calls=%fused_computation.5 | loop fusion | flops 2097152 | bytes 12582912 | tf_op jit(solution)/shard_map/convert_element_type | solution.py:164
  227.1 10.8 %scatter_fusion.1 = f32[2,2,64,1024]{3,2,1,0:T(8,128)S(1)} fusion(f32[2,2,64,1024]{3,2,1,0:T(8,128)S(1)} %broadcast_in_dim.50, s32[16]{0:T(128)S(1)} %fusion.35, f32[16,2,64,1024]{3,2,1,0:T(8,128)} %bitcast_convert_fusion), kind=kCustom, calls=%fused_computation.4 | custom fusion | flops 2097152 | bytes 25165888 | tf_op jit(solution)/shard_map/scatter-add | solution.py:164
  (156 shorter events, 65.4 us)
Async XLA Ops:
  11.0 9.8 %all-to-all-start = ((s32[8,1,2]{2,1,0:T(1,128)}), s32[8,1,2]{2,1,0:T(1,128)S(1)}, u32[]{:S(2)}, u32[]{:S(2)}) async-start(s32[8,1,2]{2,1,0:T(1,128)} %bitcast.12), calls=%async_computation | async-start | bytes 8192 | tf_op jit(solution)/shard_map/all_to_all | solution.py:134
  23.8 4.8 %copy-start.26 = (bf16[1,128,1024]{2,1,0:T(8,128)(2,1)S(1)}, bf16[1,128,1024]{2,1,0:T(8,128)(2,1)}, u32[]{:S(2)}) copy-start(bf16[1,128,1024]{2,1,0:T(8,128)(2,1)} %param.15) | copy-start | bytes 786436
  23.8 4.9 %copy-start.27 = (bf16[1,128,1024]{2,1,0:T(8,128)(2,1)S(1)}, bf16[1,128,1024]{2,1,0:T(8,128)(2,1)}, u32[]{:S(2)}) copy-start(bf16[1,128,1024]{2,1,0:T(8,128)(2,1)} %param.16) | copy-start | bytes 786436
  23.8 80.5 %all-to-all-start.1 = ((bf16[8,2,2,64,1024]{4,3,2,1,0:T(8,128)(2,1)}), bf16[8,2,2,64,1024]{4,3,2,1,0:T(8,128)(2,1)}, u32[]{:S(2)}, u32[]{:S(2)}) async-start(bf16[8,2,2,64,1024]{4,3,2,1,0:T(8,128)(2,1)} %bitcast.105), calls=%async_computation.1 | async-start | bytes 8388608 | tf_op jit(solution)/shard_map/all_to_all | solution.py:137
  28.5 3.6 %copy-start.28 = (bf16[1,128,1024]{2,1,0:T(8,128)(2,1)S(1)}, bf16[1,128,1024]{2,1,0:T(8,128)(2,1)}, u32[]{:S(2)}) copy-start(bf16[1,128,1024]{2,1,0:T(8,128)(2,1)} %param.14) | copy-start | bytes 786436
  28.6 4.0 %copy-start.25 = (bf16[1,128,1024]{2,1,0:T(8,128)(2,1)S(1)}, bf16[1,128,1024]{2,1,0:T(8,128)(2,1)}, u32[]{:S(2)}) copy-start(bf16[1,128,1024]{2,1,0:T(8,128)(2,1)} %param.18) | copy-start | bytes 786436
  28.6 4.3 %copy-start.29 = (bf16[1,128,1024]{2,1,0:T(8,128)(2,1)S(1)}, bf16[1,128,1024]{2,1,0:T(8,128)(2,1)}, u32[]{:S(2)}) copy-start(bf16[1,128,1024]{2,1,0:T(8,128)(2,1)} %param.17) | copy-start | bytes 786436
  28.6 150.4 %all-reduce.8.cloned.1.call-start = ((), (), s32[]{:S(2)}) async-start(), calls=%async_computation.3 | async-start | bytes 2097152 | tf_op jit(solution)/shard_map/psum | solution.py:109
  29.5 56.1 %collective-permute-start = (bf16[2,64,1024]{2,1,0:T(8,128)(2,1)}, bf16[2,64,1024]{2,1,0:T(8,128)(2,1)}, u32[]{:S(2)}, u32[]{:S(2)}) collective-permute-start(bf16[2,64,1024]{2,1,0:T(8,128)(2,1)} %get-tuple-element.67), channel_id=1, source_target_pairs={{0,1},{1,2},{2,3},{3,4},{4,5},{5,6},{6,7},{7,0},{8,9},{9,10},{10,1... | collective-permute-start | bytes 786440 | tf_op jit(solution)/shard_map/ppermute | solution.py:18
  29.9 55.7 %collective-permute-start.1 = (bf16[2,64,1024]{2,1,0:T(8,128)(2,1)}, bf16[2,64,1024]{2,1,0:T(8,128)(2,1)}, u32[]{:S(2)}, u32[]{:S(2)}) collective-permute-start(bf16[2,64,1024]{2,1,0:T(8,128)(2,1)} %get-tuple-element.68), channel_id=1, source_target_pairs={{1,0},{2,1},{3,2},{4,3},{5,4},{6,5},{7,6},{0,7},{9,8},{10,9},{11,1... | collective-permute-start | bytes 786440 | tf_op jit(solution)/shard_map/ppermute | solution.py:21
  32.9 67.1 %copy-start.2 = (bf16[2,64,16,64]{3,2,1,0:T(8,128)(2,1)}, bf16[2,64,16,64]{3,2,1,0:T(8,128)(2,1)S(1)}, u32[]{:S(2)}) copy-start(bf16[2,64,16,64]{3,2,1,0:T(8,128)(2,1)S(1)} %reshape.259) | copy-start | bytes 786436
  131.4 3.1 %copy-start.7 = (bf16[2,3,64,16,64]{4,2,3,1,0:T(8,128)(2,1)S(1)}, bf16[2,3,64,16,64]{4,2,3,1,0:T(8,128)(2,1)}, u32[]{:S(2)}) copy-start(bf16[2,3,64,16,64]{4,2,3,1,0:T(8,128)(2,1)} %copy-done.6) | copy-start | bytes 2359300
  135.6 2.2 copy-start.22
  145.4 5.0 %copy-start.13 = (f32[2,192,16,64]{1,3,2,0:T(8,128)S(1)}, f32[2,192,16,64]{1,3,2,0:T(8,128)}, u32[]{:S(2)}) copy-start(f32[2,192,16,64]{1,3,2,0:T(8,128)} %multiply_bitcast_fusion) | copy-start | bytes 4718596
  145.4 75.0 %all-to-all-start.2 = ((bf16[8,2,2,64,1024]{4,3,2,1,0:T(8,128)(2,1)}), bf16[8,2,2,64,1024]{4,3,2,1,0:T(8,128)(2,1)}, u32[]{:S(2)}, u32[]{:S(2)}) async-start(bf16[8,2,2,64,1024]{4,3,2,1,0:T(8,128)(2,1)} %bitcast.104), calls=%async_computation.2 | async-start | bytes 8388608 | tf_op jit(solution)/shard_map/all_to_all | solution.py:153
  153.3 2.9 %copy-start.1 = (f32[2,16,192,64]{2,3,1,0:T(8,128)S(1)}, f32[2,16,192,64]{2,3,1,0:T(8,128)}, u32[]{:S(2)}) copy-start(f32[2,16,192,64]{2,3,1,0:T(8,128)} %copy-done) | copy-start | bytes 4718596
  153.3 2.9 %copy-start.3 = (bf16[2,64,16,64]{3,2,1,0:T(8,128)(2,1)S(1)}, bf16[2,64,16,64]{3,2,1,0:T(8,128)(2,1)}, u32[]{:S(2)}) copy-start(bf16[2,64,16,64]{3,2,1,0:T(8,128)(2,1)} %copy-done.2) | copy-start | bytes 786436
  162.4 2.2 copy-start.17
  162.4 4.9 %copy-start.12 = (bf16[2,2,192,16,64]{2,4,3,1,0:T(8,128)(2,1)S(1)}, bf16[2,2,192,16,64]{2,4,3,1,0:T(8,128)(2,1)}, u32[]{:S(2)}) copy-start(bf16[2,2,192,16,64]{2,4,3,1,0:T(8,128)(2,1)} %copy-done.11) | copy-start | bytes 4718596
  162.4 4.9 %copy-start.15 = (bf16[2,16,192,64]{2,3,1,0:T(8,128)(2,1)S(1)}, bf16[2,16,192,64]{2,3,1,0:T(8,128)(2,1)}, u32[]{:S(2)}) copy-start(bf16[2,16,192,64]{2,3,1,0:T(8,128)(2,1)} %copy-done.14) | copy-start | bytes 2359300
  164.7 47.5 %collective-permute-start.2 = (f32[2,64,1024]{2,1,0:T(8,128)}, f32[2,64,1024]{2,1,0:T(8,128)}, u32[]{:S(2)}, u32[]{:S(2)}) collective-permute-start(f32[2,64,1024]{2,1,0:T(8,128)} %get-tuple-element.52), channel_id=1, source_target_pairs={{0,1},{1,2},{2,3},{3,4},{4,5},{5,6},{6,7},{7,0},{8,9},{9,10},{10,1... | collective-permute-start | bytes 1572872 | tf_op jit(solution)/shard_map/ppermute | solution.py:18
  164.8 49.4 %collective-permute-start.3 = (f32[2,64,1024]{2,1,0:T(8,128)}, f32[2,64,1024]{2,1,0:T(8,128)}, u32[]{:S(2)}, u32[]{:S(2)}) collective-permute-start(f32[2,64,1024]{2,1,0:T(8,128)} %get-tuple-element.51), channel_id=1, source_target_pairs={{1,0},{2,1},{3,2},{4,3},{5,4},{6,5},{7,6},{0,7},{9,8},{10,9},{11,1... | collective-permute-start | bytes 1572872 | tf_op jit(solution)/shard_map/ppermute | solution.py:21
  182.1 34.3 %copy-start.5 = (bf16[6,1,64,16,64]{4,3,2,1,0:T(8,128)(2,1)S(1)}, bf16[6,1,64,16,64]{4,3,2,1,0:T(8,128)(2,1)}, u32[]{:S(2)}) copy-start(bf16[6,1,64,16,64]{4,3,2,1,0:T(8,128)(2,1)} %copy-done.4) | copy-start | bytes 2359300
  182.1 34.3 %copy-start.9 = (bf16[6,16,64,64]{3,2,1,0:T(8,128)(2,1)S(1)}, bf16[6,16,64,64]{3,2,1,0:T(8,128)(2,1)}, u32[]{:S(2)}) copy-start(bf16[6,16,64,64]{3,2,1,0:T(8,128)(2,1)} %copy-done.8) | copy-start | bytes 2359300
  (15 other events, 19.4 us)
Sparse Core Ops, SparseCore 0:
  39.0 139.9 all-reduce.7
where the time goes:
time: 248 us; the launch traced here: 247 us
  local copies, waits for them, and re-layouts  84.7 us (34%)
  waiting for transfers between devices  81.6 us (33%)
  other arithmetic  32.2 us (13%)
  starting transfers between devices  20.2 us (8%)
  between operations  14.7 us (6%)
  matrix products  13.6 us (5%)
    ppermute x2, waiting for transfers between devices, extended(): lax.ppermute(lax.slice_in_dim(block, block.shape[dim] - width, None, axis...  67.8 us
    reshape x6, local copies, waits for them, and re-layouts, split_blocks(): return section.reshape(2, blocks, BLK, HEADS, HDIM)  13.2 us
    reshape x1, local copies, waits for them, and re-layouts, shards(): chosen = fetched.reshape(slots_all, 2, BLK, HEADS, HDIM)[slot_index]  11.6 us
    unnamed x68, local copies, waits for them, and re-layouts  11.1 us
    scatter-add x1, other arithmetic, shards(): kv_rand = jnp.zeros((blocks, 2, BLK, feature_dim), jnp.float32).at[asked_...  10.8 us
    psum x1, waiting for transfers between devices, shards(): memory_total = lax.psum(mem_terms, ('dp', 'ctx'))  10.2 us
    convert_element_type x1, other arithmetic, shards(): received.astype(jnp.float32)  6.53 us
    all_to_all x1, starting transfers between devices, shards(): lax.all_to_all(wanted, 'ctx', split_axis=0, concat_axis=0, tiled=True)  5.17 us
  transfers between devices with their start and end apart: 8, of which 4 were waited for; matrix products, arithmetic and copies ran while one was open for 40% of the time, Pallas kernels for 0%

commit v1 on v0

--- a/solution.py
+++ b/solution.py
@@ -106,7 +106,7 @@
     mem_terms = jnp.stack([jnp.sum(dk_mem, axis=0), jnp.sum(dv_mem, axis=0)]).reshape(
         2, GLOB, feature_dim
     )
-    memory_total = lax.psum(mem_terms, ("dp", "ctx"))
+    memory_total = lax.psum(lax.psum(mem_terms, "ctx"), "dp")
     capacity = min(blocks, max(2, 2 * blocks * per_block // cycle_size))
     owner_flat = rand_owner.reshape(-1)
     local_flat = rand_local.reshape(-1)

time: 248 us -> 261 us (1.052)
  waiting for transfers between devices: 81.6 us -> 88.8 us
  local copies, waits for them, and re-layouts: 84.7 us -> 89.2 us
    ppermute x2, waiting for transfers between devices: 67.8 us -> 79.5 us  [extended(): lax.ppermute(lax.slice_in_dim(block, block.shape[dim] - width, None, axis...]
    psum x1 -> x2, waiting for transfers between devices: 10.2 us -> 5.67 us  [shards(): memory_total = lax.psum(lax.psum(mem_terms, 'ctx'), 'dp')]
    unnamed x68 -> x66, local copies, waits for them, and re-layouts: 11.1 us -> 12.4 us
  transfers between devices with their start and end apart: 8 -> 9, of which waited for: 4 -> 4; matrix products, arithmetic and copies ran while one was open for 40% -> 40% of each run, Pallas kernels for 0% -> 0%
where the time goes in v1:
time: 261 us; the launch traced here: 260 us
  local copies, waits for them, and re-layouts  89.2 us (34%)
  waiting for transfers between devices  88.8 us (34%)
  other arithmetic  34.8 us (13%)
  starting transfers between devices  20 us (8%)
  between operations  14.7 us (6%)
  matrix products  12.2 us (5%)
    ppermute x2, waiting for transfers between devices, extended(): lax.ppermute(lax.slice_in_dim(block, block.shape[dim] - width, None, axis...  79.5 us
    reshape x6, local copies, waits for them, and re-layouts, split_blocks(): return section.reshape(2, blocks, BLK, HEADS, HDIM)  13.2 us
    unnamed x66, local copies, waits for them, and re-layouts  12.4 us
    reshape x1, local copies, waits for them, and re-layouts, shards(): chosen = fetched.reshape(slots_all, 2, BLK, HEADS, HDIM)[slot_index]  11.6 us
    scatter-add x1, other arithmetic, shards(): kv_rand = jnp.zeros((blocks, 2, BLK, feature_dim), jnp.float32).at[asked_...  10.8 us
    convert_element_type x1, other arithmetic, shards(): received.astype(jnp.float32)  6.51 us
    psum x2, waiting for transfers between devices, shards(): memory_total = lax.psum(lax.psum(mem_terms, 'ctx'), 'dp')  5.67 us
  transfers between devices with their start and end apart: 9, of which 4 were waited for; matrix products, arithmetic and copies ran while one was open for 40% of the time, Pallas kernels for 0%

profile of v1, /device:TPU:0, one launch (start us, length us, event | category | flops | bytes accessed | tf_op | source)
XLA Modules:
  0.0 259.7 jit_solution(13702558287147630870)
XLA Ops:
  11.0 5.2 %all-to-all-start = ((s32[8,1,2]{2,1,0:T(1,128)}), s32[8,1,2]{2,1,0:T(1,128)S(1)}, u32[]{:S(2)}, u32[]{:S(2)}) async-start(s32[8,1,2]{2,1,0:T(1,128)} %bitcast.12), calls=%async_computation | async-start | bytes 8192 | tf_op jit(solution)/shard_map/all_to_all | solution.py:134
  17.3 3.5 %all-to-all-done = s32[8,1,2]{2,1,0:T(1,128)S(1)} async-done(((s32[8,1,2]{2,1,0:T(1,128)}), s32[8,1,2]{2,1,0:T(1,128)S(1)}, u32[]{:S(2)}, u32[]{:S(2)}) %all-to-all-start) | async-done | bytes 96 | tf_op jit(solution)/shard_map/all_to_all | solution.py:134
  21.0 2.8 %gather_fusion = bf16[16,2,64,1024]{3,2,1,0:T(8,128)(2,1)} fusion(bf16[2,2,64,1024]{3,2,0,1:T(8,128)(2,1)S(1)} %pad_maximum_fusion.5, s32[1024]{0:T(1024)S(1)} %pad_clamp_fusion.1), kind=kCustom, calls=%fused_computation | custom fusion | bytes 8388672 | tf_op jit(solution)/shard_map/gather | solution.py:135
  23.8 4.8 %all-to-all-start.1 = ((bf16[8,2,2,64,1024]{4,3,2,1,0:T(8,128)(2,1)}), bf16[8,2,2,64,1024]{4,3,2,1,0:T(8,128)(2,1)}, u32[]{:S(2)}, u32[]{:S(2)}) async-start(bf16[8,2,2,64,1024]{4,3,2,1,0:T(8,128)(2,1)} %bitcast.105), calls=%async_computation.1 | async-start | bytes 8388608 | tf_op jit(solution)/shard_map/all_to_all | solution.py:137
  29.9 2.3 collective-permute-start.1
  46.4 42.0 %collective-permute-done = bf16[2,64,1024]{2,1,0:T(8,128)(2,1)} collective-permute-done((bf16[2,64,1024]{2,1,0:T(8,128)(2,1)}, bf16[2,64,1024]{2,1,0:T(8,128)(2,1)}, u32[]{:S(2)}, u32[]{:S(2)}) %collective-permute-start) | collective-permute-done | bytes 262176 | tf_op jit(solution)/shard_map/ppermute | solution.py:18
  90.3 2.5 reshape.256
  92.8 2.7 %copy.130 = bf16[2,2,64,16,64]{2,4,3,1,0:T(8,128)(2,1)} copy(bf16[2,2,64,16,64]{4,3,2,1,0:T(8,128)(2,1)} %reshape.256) | data formatting | bytes 1048576 | tf_op jit(solution)/shard_map/reshape | solution.py:76
  97.2 2.7 %copy.128 = bf16[2,2,64,16,64]{2,4,3,1,0:T(8,128)(2,1)} copy(bf16[2,2,64,16,64]{4,3,2,1,0:T(8,128)(2,1)} %reshape.254) | data formatting | bytes 1048576 | tf_op jit(solution)/shard_map/reshape | solution.py:76
  99.9 2.6 pad_maximum_fusion
  107.4 11.6 %reshape.262 = bf16[16,2,64,16,64]{4,3,2,1,0:T(8,128)(2,1)} reshape(bf16[8,2,2,64,1024]{4,3,2,1,0:T(8,128)(2,1)} %all-to-all-done.1) | data formatting | bytes 8388608 | tf_op jit(solution)/shard_map/reshape | solution.py:140
  119.0 4.5 %gather_fusion.1 = bf16[6,2,64,16,64]{4,3,2,1,0:T(8,128)(2,1)S(1)} fusion(bf16[16,2,64,16,64]{4,3,2,1,0:T(8,128)(2,1)} %reshape.262, s32[1024]{0:T(1024)S(1)} %pad_clamp_fusion), kind=kCustom, calls=%fused_computation.1 | custom fusion | bytes 3145752 | tf_op jit(solution)/shard_map/gather | solution.py:140
  131.0 3.4 %stack.39 = bf16[6,1,64,1024]{3,2,0,1:T(8,128)(2,1)} reshape(bf16[6,64,16,64]{3,2,1,0:T(8,128)(2,1)} %copy.156) | data formatting | bytes 1572864 | tf_op jit(solution)/shard_map/stack | solution.py:146
  134.4 3.0 %multiply_convert_fusion.2 = bf16[6,16,64,64]{3,2,1,0:T(8,128)(2,1)S(1)} fusion(f32[6,16,64,64]{3,2,1,0:T(8,128)S(1)} %fusion.10, bf16[6,64,16,64]{3,1,2,0:T(8,128)(2,1)} %bitcast.109, bf16[6,1,64,16,64]{4,3,2,1,0:T(8,128)(2,1)} %get-tuple-element.49, f32[6,16,64]{2,1,0:T(8,128)S(1)} %bitcast.127, f32[6,16,64]{2,1,0:T(8,128)S(1)} %bitcast.121), kind=kOutput, calls=%fused_computation.9 | convolution fusion | flops 52297728 | bytes 3981312 | tf_op jit(solution)/shard_map/nqhe,nkhe->nhqk/dot_general | solution.py:34
  141.2 2.5 broadcast_in_dim.51
  143.6 4.8 %scatter_fusion = bf16[16,2,64,1024]{3,2,1,0:T(8,128)(2,1)} fusion(bf16[16,2,64,1024]{3,2,1,0:T(8,128)(2,1)} %broadcast_in_dim.51, s32[6]{0:T(128)S(1)} %fusion.34, bf16[6,2,64,1024]{3,2,1,0:T(8,128)(2,1)S(1)} %copy.157), kind=kCustom, calls=%fused_computation.3 | custom fusion | bytes 4718616 | tf_op jit(solution)/shard_map/scatter | solution.py:151
  148.5 4.8 %all-to-all-start.2 = ((bf16[8,2,2,64,1024]{4,3,2,1,0:T(8,128)(2,1)}), bf16[8,2,2,64,1024]{4,3,2,1,0:T(8,128)(2,1)}, u32[]{:S(2)}, u32[]{:S(2)}) async-start(bf16[8,2,2,64,1024]{4,3,2,1,0:T(8,128)(2,1)} %bitcast.104), calls=%async_computation.2 | async-start | bytes 8388608 | tf_op jit(solution)/shard_map/all_to_all | solution.py:153
  157.4 2.9 %stack.35 = f32[1,256,1024]{2,1,0:T(8,128)} reshape(f32[4,64,16,64]{3,2,1,0:T(8,128)} %copy.152) | data formatting | bytes 2097152 | tf_op jit(solution)/shard_map/stack | solution.py:89
  169.3 2.5 slice.161
  171.8 2.3 collective-permute-start.3
  175.5 37.6 %collective-permute-done.2 = f32[2,64,1024]{2,1,0:T(8,128)} collective-permute-done((f32[2,64,1024]{2,1,0:T(8,128)}, f32[2,64,1024]{2,1,0:T(8,128)}, u32[]{:S(2)}, u32[]{:S(2)}) %collective-permute-start.2) | collective-permute-done | bytes 524320 | tf_op jit(solution)/shard_map/ppermute | solution.py:18
  217.2 5.7 %all-reduce.11.cloned.1.call-done = f32[2,128,1024]{1,2,0:T(8,128)} async-done(((f32[2,128,1024]{1,2,0:T(8,128)}), f32[2,128,1024]{1,2,0:T(8,128)}) %all-reduce.11.cloned.1.call-update) | async-done | bytes 1048592 | tf_op jit(solution)/shard_map/psum | solution.py:109
  233.2 6.5 %bitcast_convert_fusion = f32[16,2,64,1024]{3,2,1,0:T(8,128)} fusion(bf16[8,2,2,64,1024]{4,3,2,1,0:T(8,128)(2,1)} %all-to-all-done.2), kind=kLoop, calls=%fused_computation.5 | loop fusion | flops 2097152 | bytes 12582912 | tf_op jit(solution)/shard_map/convert_element_type | solution.py:164
  239.8 10.8 %scatter_fusion.1 = f32[2,2,64,1024]{3,2,1,0:T(8,128)S(1)} fusion(f32[2,2,64,1024]{3,2,1,0:T(8,128)S(1)} %broadcast_in_dim.50, s32[16]{0:T(128)S(1)} %fusion.35, f32[16,2,64,1024]{3,2,1,0:T(8,128)} %bitcast_convert_fusion), kind=kCustom, calls=%fused_computation.4 | custom fusion | flops 2097152 | bytes 25165888 | tf_op jit(solution)/shard_map/scatter-add | solution.py:164
  (157 shorter events, 71.2 us)
Async XLA Ops:
  11.0 9.8 %all-to-all-start = ((s32[8,1,2]{2,1,0:T(1,128)}), s32[8,1,2]{2,1,0:T(1,128)S(1)}, u32[]{:S(2)}, u32[]{:S(2)}) async-start(s32[8,1,2]{2,1,0:T(1,128)} %bitcast.12), calls=%async_computation | async-start | bytes 8192 | tf_op jit(solution)/shard_map/all_to_all | solution.py:134
  23.8 4.9 %copy-start.25 = (bf16[1,128,1024]{2,1,0:T(8,128)(2,1)S(1)}, bf16[1,128,1024]{2,1,0:T(8,128)(2,1)}, u32[]{:S(2)}) copy-start(bf16[1,128,1024]{2,1,0:T(8,128)(2,1)} %param.15) | copy-start | bytes 786436
  23.8 4.9 %copy-start.26 = (bf16[1,128,1024]{2,1,0:T(8,128)(2,1)S(1)}, bf16[1,128,1024]{2,1,0:T(8,128)(2,1)}, u32[]{:S(2)}) copy-start(bf16[1,128,1024]{2,1,0:T(8,128)(2,1)} %param.16) | copy-start | bytes 786436
  23.8 83.6 %all-to-all-start.1 = ((bf16[8,2,2,64,1024]{4,3,2,1,0:T(8,128)(2,1)}), bf16[8,2,2,64,1024]{4,3,2,1,0:T(8,128)(2,1)}, u32[]{:S(2)}, u32[]{:S(2)}) async-start(bf16[8,2,2,64,1024]{4,3,2,1,0:T(8,128)(2,1)} %bitcast.105), calls=%async_computation.1 | async-start | bytes 8388608 | tf_op jit(solution)/shard_map/all_to_all | solution.py:137
  28.6 3.6 %copy-start.27 = (bf16[1,128,1024]{2,1,0:T(8,128)(2,1)S(1)}, bf16[1,128,1024]{2,1,0:T(8,128)(2,1)}, u32[]{:S(2)}) copy-start(bf16[1,128,1024]{2,1,0:T(8,128)(2,1)} %param.14) | copy-start | bytes 786436
  28.6 4.0 %copy-start.24 = (bf16[1,128,1024]{2,1,0:T(8,128)(2,1)S(1)}, bf16[1,128,1024]{2,1,0:T(8,128)(2,1)}, u32[]{:S(2)}) copy-start(bf16[1,128,1024]{2,1,0:T(8,128)(2,1)} %param.18) | copy-start | bytes 786436
  28.6 4.3 %copy-start.28 = (bf16[1,128,1024]{2,1,0:T(8,128)(2,1)S(1)}, bf16[1,128,1024]{2,1,0:T(8,128)(2,1)}, u32[]{:S(2)}) copy-start(bf16[1,128,1024]{2,1,0:T(8,128)(2,1)} %param.17) | copy-start | bytes 786436
  28.6 140.6 %all-reduce.9.cloned.1.call-start = ((), (), s32[]{:S(2)}) async-start(), calls=%async_computation.3 | async-start | bytes 2097152 | tf_op jit(solution)/shard_map/psum | solution.py:109
  29.5 58.9 %collective-permute-start = (bf16[2,64,1024]{2,1,0:T(8,128)(2,1)}, bf16[2,64,1024]{2,1,0:T(8,128)(2,1)}, u32[]{:S(2)}, u32[]{:S(2)}) collective-permute-start(bf16[2,64,1024]{2,1,0:T(8,128)(2,1)} %get-tuple-element.67), channel_id=1, source_target_pairs={{0,1},{1,2},{2,3},{3,4},{4,5},{5,6},{6,7},{7,0},{8,9},{9,10},{10,1... | collective-permute-start | bytes 786440 | tf_op jit(solution)/shard_map/ppermute | solution.py:18
  29.9 58.5 %collective-permute-start.1 = (bf16[2,64,1024]{2,1,0:T(8,128)(2,1)}, bf16[2,64,1024]{2,1,0:T(8,128)(2,1)}, u32[]{:S(2)}, u32[]{:S(2)}) collective-permute-start(bf16[2,64,1024]{2,1,0:T(8,128)(2,1)} %get-tuple-element.68), channel_id=1, source_target_pairs={{1,0},{2,1},{3,2},{4,3},{5,4},{6,5},{7,6},{0,7},{9,8},{10,9},{11,1... | collective-permute-start | bytes 786440 | tf_op jit(solution)/shard_map/ppermute | solution.py:21
  32.9 70.0 %copy-start.2 = (bf16[2,64,16,64]{3,2,1,0:T(8,128)(2,1)}, bf16[2,64,16,64]{3,2,1,0:T(8,128)(2,1)S(1)}, u32[]{:S(2)}) copy-start(bf16[2,64,16,64]{3,2,1,0:T(8,128)(2,1)S(1)} %reshape.259) | copy-start | bytes 786436
  134.4 3.0 %copy-start.7 = (bf16[2,3,64,16,64]{4,2,3,1,0:T(8,128)(2,1)S(1)}, bf16[2,3,64,16,64]{4,2,3,1,0:T(8,128)(2,1)}, u32[]{:S(2)}) copy-start(bf16[2,3,64,16,64]{4,2,3,1,0:T(8,128)(2,1)} %copy-done.6) | copy-start | bytes 2359300
  138.6 2.2 copy-start.21
  148.5 4.8 %copy-start.20 = (f32[2,64,16,64]{1,3,2,0:T(8,128)S(1)}, f32[2,64,16,64]{1,3,2,0:T(8,128)}, u32[]{:S(2)}) copy-start(f32[2,64,16,64]{1,3,2,0:T(8,128)} %get-tuple-element.56) | copy-start | bytes 1572868
  148.5 84.7 %all-to-all-start.2 = ((bf16[8,2,2,64,1024]{4,3,2,1,0:T(8,128)(2,1)}), bf16[8,2,2,64,1024]{4,3,2,1,0:T(8,128)(2,1)}, u32[]{:S(2)}, u32[]{:S(2)}) async-start(bf16[8,2,2,64,1024]{4,3,2,1,0:T(8,128)(2,1)} %bitcast.104), calls=%async_computation.2 | async-start | bytes 8388608 | tf_op jit(solution)/shard_map/all_to_all | solution.py:153
  153.2 69.6 %all-reduce.11.cloned.1.call-start = ((), (), s32[]{:S(2)}) async-start(), calls=%async_computation.4 | async-start | bytes 2097152 | tf_op jit(solution)/shard_map/psum | solution.py:109
  157.4 2.9 %copy-start.1 = (f32[2,16,192,64]{2,3,1,0:T(8,128)S(1)}, f32[2,16,192,64]{2,3,1,0:T(8,128)}, u32[]{:S(2)}) copy-start(f32[2,16,192,64]{2,3,1,0:T(8,128)} %copy-done) | copy-start | bytes 4718596
  157.4 2.9 %copy-start.3 = (bf16[2,64,16,64]{3,2,1,0:T(8,128)(2,1)S(1)}, bf16[2,64,16,64]{3,2,1,0:T(8,128)(2,1)}, u32[]{:S(2)}) copy-start(bf16[2,64,16,64]{3,2,1,0:T(8,128)(2,1)} %copy-done.2) | copy-start | bytes 786436
  168.9 5.2 %copy-start.12 = (bf16[2,2,192,16,64]{2,4,3,1,0:T(8,128)(2,1)S(1)}, bf16[2,2,192,16,64]{2,4,3,1,0:T(8,128)(2,1)}, u32[]{:S(2)}) copy-start(bf16[2,2,192,16,64]{2,4,3,1,0:T(8,128)(2,1)} %copy-done.11) | copy-start | bytes 4718596
  168.9 5.2 %copy-start.14 = (bf16[2,16,192,64]{2,3,1,0:T(8,128)(2,1)S(1)}, bf16[2,16,192,64]{2,3,1,0:T(8,128)(2,1)}, u32[]{:S(2)}) copy-start(bf16[2,16,192,64]{2,3,1,0:T(8,128)(2,1)} %copy-done.13) | copy-start | bytes 2359300
  168.9 44.2 %collective-permute-start.2 = (f32[2,64,1024]{2,1,0:T(8,128)}, f32[2,64,1024]{2,1,0:T(8,128)}, u32[]{:S(2)}, u32[]{:S(2)}) collective-permute-start(f32[2,64,1024]{2,1,0:T(8,128)} %get-tuple-element.52), channel_id=1, source_target_pairs={{0,1},{1,2},{2,3},{3,4},{4,5},{5,6},{6,7},{7,0},{8,9},{9,10},{10,1... | collective-permute-start | bytes 1572872 | tf_op jit(solution)/shard_map/ppermute | solution.py:18
  171.8 43.4 %collective-permute-start.3 = (f32[2,64,1024]{2,1,0:T(8,128)}, f32[2,64,1024]{2,1,0:T(8,128)S(1)}, u32[]{:S(2)}, u32[]{:S(2)}) collective-permute-start(f32[2,64,1024]{2,1,0:T(8,128)} %get-tuple-element.51), channel_id=1, source_target_pairs={{1,0},{2,1},{3,2},{4,3},{5,4},{6,5},{7,6},{0,7},{9,8},{10,9},{11,1... | collective-permute-start | bytes 1572872 | tf_op jit(solution)/shard_map/ppermute | solution.py:21
  217.2 12.0 %copy-start.5 = (bf16[6,1,64,16,64]{4,3,2,1,0:T(8,128)(2,1)S(1)}, bf16[6,1,64,16,64]{4,3,2,1,0:T(8,128)(2,1)}, u32[]{:S(2)}) copy-start(bf16[6,1,64,16,64]{4,3,2,1,0:T(8,128)(2,1)} %copy-done.4) | copy-start | bytes 2359300
  217.2 12.0 %copy-start.9 = (bf16[6,16,64,64]{3,2,1,0:T(8,128)(2,1)S(1)}, bf16[6,16,64,64]{3,2,1,0:T(8,128)(2,1)}, u32[]{:S(2)}) copy-start(bf16[6,16,64,64]{3,2,1,0:T(8,128)(2,1)} %copy-done.8) | copy-start | bytes 2359300
  (15 other events, 19.5 us)
Sparse Core Ops, SparseCore 0:
  39.8 73.2 all-reduce.8
  169.4 53.4 all-reduce.10
